TPU v7x, 32 devices: a whole 2x2x4 slice. The times are simulated.
32 devices in a mesh: slab: 16 (over z, y, x), sub: 2 (over core).
Axes of the slice: x: 2, y: 2, z: 4, core: 2. Of those that a mesh axis runs over, the one named last changes fastest.
Arguments:
- velocities: float32 [3, 163840], P(None, ('slab', 'sub')), may hold values from -16 to 19
- cell_index: int32 [1, 163840], P(None, ('slab', 'sub')), may hold values from 0 to 511
- axis_choice: int32 [1, 16384], P(None, ('slab', 'sub')), may hold values from 0 to 63
- moves: int32 [1, 4, 4096], P(None, None, ('slab', 'sub')), may hold values from 0 to 5119, as said below
- shear_target: float32 [128], P('sub'), may hold values from -6 to 6
Outputs:
- velocities_final: float32 [3, 163840], P(None, ('slab', 'sub'))
- profile: float32 [16, 128], P('slab', 'sub')
Inputs may be any that keep to these rules, and one draw needn't show every extreme that they name: `moves`: in each step the 512 slots of one device's four lists are distinct.
All inputs are finite; a program needn't handle non-finite values.
Results may differ from a plain program's by a relative error of at most 0.0003.
Values sent between devices are 32-bit elements; how exact they have to be, the bound alone decides.
No kernel may reach another device: no remote copies, remote signals or barrier semaphores. Data moves between devices by JAX's collectives and lax.ppermute only.
A program may use at most 64 MiB of HBM per device.

v0:
```python
import jax
import jax.numpy as jnp
from jax import lax
from jax.sharding import PartitionSpec as P

CX = 1
CY = 64
CZ = 8
NAXES = 64
ROT_COS = -0.6427876096865393
ROT_SIN = 0.766044443118978
RESERVOIR_HEAT = 0.9
FEEDBACK = 1.0
GOLDEN = 2.399963229728653


def from_behind(block, axis, distance):
    devices = range(lax.axis_size(axis))
    route = [((i - distance) % len(devices), i) for i in devices]
    return lax.ppermute(block, axis, route)


def axis_table():
    counter = jnp.arange(NAXES, dtype=jnp.int32).astype(jnp.float32)
    height = 1.0 - (2.0 * counter + 1.0) / NAXES
    radius = jnp.sqrt(1.0 - height * height)
    return jnp.stack(
        [radius * jnp.cos(GOLDEN * counter), radius * jnp.sin(GOLDEN * counter), height]
    )


def bin_cells(values, weights, cells, totals):
    stacked = jnp.concatenate([values, weights[None, :]], 0)
    return totals.at[:, cells].add(stacked)


def cell_state(totals, choices, table):
    counts = jnp.maximum(totals[3], 1.0)
    average_value = totals[:3] / counts
    onehot = (jnp.arange(NAXES, dtype=jnp.int32)[:, None] == choices[None, :]).astype(jnp.float32)
    axes = jnp.dot(table, onehot, precision=lax.Precision.HIGHEST)
    columns = jnp.sum(totals.reshape(4, CX * CY, CZ), 2)
    block = (columns[0] / jnp.maximum(columns[3], 1.0)).reshape(CX, CY)
    return (average_value, axes, block)


def collide(relative, cells, average_value, axes, speed_multiplier, adjustment_factor):
    normal = axes[:, cells]
    cross = jnp.stack(
        [
            normal[1] * relative[2] - normal[2] * relative[1],
            normal[2] * relative[0] - normal[0] * relative[2],
            normal[0] * relative[1] - normal[1] * relative[0],
        ]
    )
    along = jnp.sum(normal * relative, 0)
    rotated = relative * ROT_COS + cross * ROT_SIN + normal * (along * (1.0 - ROT_COS))
    shifted = average_value.at[0].add(adjustment_factor)
    return shifted[:, cells] + speed_multiplier * rotated


def body(velocities, cell_index, axis_choice, moves, shear_target):
    speeds = velocities
    slabs = lax.axis_size("slab")
    sub_count = lax.axis_size("sub")
    inner_position = lax.axis_index("sub")
    count_here = speeds.shape[1]
    whole_swarm = count_here * slabs * sub_count
    width_x = CX * slabs
    block_rows = moves.shape[2]
    table = axis_table()
    slots = moves[0].reshape(-1)
    cells = cell_index[0]
    outgoing = speeds[:, slots].reshape(3, 4, block_rows)
    weights = jnp.ones((count_here,), jnp.float32)
    empty = jnp.zeros((4, CX * CY * CZ), jnp.float32)
    east_in = from_behind(outgoing[:, 1], "slab", -1)
    west_in = from_behind(outgoing[:, 0], "slab", 1)
    north_incoming = from_behind(outgoing[:, 3], "sub", -1)
    south_in = from_behind(outgoing[:, 2], "sub", 1)
    arriving = jnp.stack([east_in, west_in, north_incoming, south_in], 1).reshape(3, 4 * block_rows)
    speeds = speeds.at[:, slots].set(arriving)
    totals = bin_cells(speeds, weights, cells, empty)
    average_value, axes, profile = cell_state(totals, axis_choice[0], table)
    relative = speeds - average_value[:, cells]
    local_energy = jnp.sum(relative * relative)
    line_aggregate = jnp.sum(profile, 0)
    padded = lax.dynamic_update_slice(
        jnp.zeros((CY * sub_count,), jnp.float32), line_aggregate, (inner_position * CY,)
    )
    summed, motion_work = lax.psum((padded, local_energy), ("slab", "sub"))
    column_sum = lax.dynamic_slice(summed, (inner_position * CY,), (CY,))
    speed_multiplier = lax.rsqrt(motion_work / (3.0 * whole_swarm * RESERVOIR_HEAT) + 1e-06)
    adjustment_factor = FEEDBACK * (shear_target - column_sum / width_x)
    per_cell = jnp.broadcast_to(adjustment_factor[None, :, None], (CX, CY, CZ)).reshape(-1)
    speeds = collide(relative, cells, average_value, axes, speed_multiplier, per_cell)
    return (speeds, profile)


def solution(mesh):
    in_specs = (
        P(None, ("slab", "sub")),
        P(None, ("slab", "sub")),
        P(None, ("slab", "sub")),
        P(None, None, ("slab", "sub")),
        P("sub"),
    )
    out_specs = (P(None, ("slab", "sub")), P("slab", "sub"))
    return jax.shard_map(body, mesh=mesh, in_specs=in_specs, out_specs=out_specs, check_vma=False)
```

profile of v0, /device:TPU:0, one launch (start us, length us, event | category | flops | bytes accessed | tf_op | source)
XLA Modules:
  0.0 134.7 jit_solution(16117041994723011014)
XLA Ops:
  0.7 1.7 %copy.103 = f32[3,5120]{0,1:T(8,128)S(1)} copy(f32[3,5120]{1,0:T(4,128)} %param.7) | data formatting | bytes 122880 | tf_op args[0]
  2.4 1.0 gather_fusion
  3.4 0.1 copy.117
  3.5 0.5 collective-permute-start.3
  4.2 3.0 %collective-permute-start.1 = (f32[3,128]{1,0:T(4,128)S(1)}, f32[3,128]{1,0:T(4,128)S(1)}, u32[]{:S(2)}, u32[]{:S(2)}) collective-permute-start(f32[3,128]{1,0:T(4,128)S(1)} %bitcast.41), channel_id=1, source_target_pairs={{30,0},{0,2},{2,4},{4,6},{6,8},{8,10},{10,12},{12,14},{14,16},{16,... | collective-permute-start | bytes 4616 | tf_op jit(solution)/shard_map/ppermute | solution.py:20
  7.2 4.0 %collective-permute-start = (f32[3,128]{1,0:T(4,128)S(1)}, f32[3,128]{1,0:T(4,128)S(1)}, u32[]{:S(2)}, u32[]{:S(2)}) collective-permute-start(f32[3,128]{1,0:T(4,128)S(1)} %bitcast.42), channel_id=1, source_target_pairs={{2,0},{4,2},{6,4},{8,6},{10,8},{12,10},{14,12},{16,14},{18,16},{20... | collective-permute-start | bytes 4616 | tf_op jit(solution)/shard_map/ppermute | solution.py:20
  11.4 0.4 fusion.5
  11.8 17.7 %gather_fusion.3 = f32[5120,3]{1,0:T(8,128)} fusion(f32[3,512]{0,1:T(8,128)S(1)} %fusion.5, s32[5120]{0:T(1024)S(1)} %broadcast_clamp_fusion), kind=kCustom, calls=%fused_computation.3 | custom fusion | bytes 143360 | tf_op jit(solution)/shard_map/gather | solution.py:48
  29.4 2.5 %copy.111 = f32[5120,3]{0,1:T(4,128)S(1)} copy(f32[5120,3]{1,0:T(8,128)} %gather_fusion.3) | data formatting | bytes 122880 | tf_op jit(solution)/shard_map/gather | solution.py:48
  32.0 0.1 copy.113
  32.2 2.7 %scatter_fusion = f32[3,5120]{0,1:T(8,128)S(1)} fusion(f32[3,5120]{0,1:T(8,128)S(1)} %copy.103, s32[512]{0:T(512)S(1)} %bitcast.37, f32[512,3]{1,0:T(8,128)S(1)} %bitcast.33), kind=kCustom, calls=%fused_computation.4 | custom fusion | bytes 20480 | tf_op jit(solution)/shard_map/scatter | solution.py:82
  34.9 0.8 copy.109
  35.6 27.9 %scatter_custom_fusion.1 = f32[4,512]{0,1:T(8,128)S(1)} fusion(s32[5120]{0:T(1024)S(1)} %bitcast.35, f32[3,5120]{0,1:T(8,128)S(1)} %scatter_fusion, f32[]{:T(128)} %constant.59.clone.1, f32[]{:T(128)} %constant.55.clone.1), kind=kCustom, calls=%fused_computation.6 | custom fusion | flops 20480 | bytes 2629640 | tf_op jit(solution)/shard_map/scatter-add | solution.py:34
  63.6 0.2 fusion.3
  63.8 0.1 bitcast_reduce_fusion
  63.9 0.1 slice_divide_fusion
  64.0 13.4 %gather_fusion.2 = f32[5120,3]{1,0:T(8,128)S(1)} fusion(f32[3,512]{0,1:T(8,128)S(1)} %slice_divide_fusion, s32[5120]{0:T(1024)S(1)} %broadcast_clamp_fusion), kind=kCustom, calls=%fused_computation.2 | custom fusion | bytes 143360 | tf_op jit(solution)/shard_map/gather | solution.py:85
  77.5 0.8 copy.108
  78.3 0.1 fusion.18
  78.3 0.1 copy.118
  78.4 0.1 copy.119
  78.5 0.7 multiply_reduce_fusion.1
  79.2 0.5 bitcast_dynamic-update-slice_fusion
  79.7 38.0 %all-reduce.1 = (f32[128]{0:T(128)S(1)}, f32[]{:T(128)}) all-reduce(f32[128]{0:T(128)S(1)} %get-tuple-element.29, f32[]{:T(128)} %get-tuple-element.24), channel_id=1, replica_groups=mesh['slab'=16,'sub'=2] {'slab','sub'}, use_global_device_ids=true, to_apply=%region_3.0 | all-reduce | flops 129 | bytes 1032 | tf_op jit(solution)/shard_map/psum | solution.py:91
  117.7 0.1 multiply_subtract_fusion.4
  117.8 0.1 broadcast_in_dim.10
  117.8 0.1 broadcast_in_dim.12
  118.0 0.9 scatter-add.13
  118.9 13.4 %gather_fusion.1 = f32[5120,3]{1,0:T(8,128)S(1)} fusion(f32[3,512]{0,1:T(8,128)S(1)} %scatter-add.13, s32[5120]{0:T(1024)S(1)} %broadcast_clamp_fusion), kind=kCustom, calls=%fused_computation.1 | custom fusion | bytes 143360 | tf_op jit(solution)/shard_map/gather | solution.py:59
  132.4 0.8 copy.107
  133.8 0.1 multiply_subtract_fusion.2
  133.9 0.7 fusion.9
  (31 shorter events, 0.4 us)
Async XLA Ops:
  0.6 1.7 %copy-start.2 = (s32[1,4,128]{2,1,0:T(4,128)S(1)}, s32[1,4,128]{2,1,0:T(4,128)}, u32[]{:S(2)}) copy-start(s32[1,4,128]{2,1,0:T(4,128)} %param.10) | copy-start | bytes 6148
  0.6 10.7 %copy-start = (s32[1,5120]{1,0:T(1,128)S(1)}, s32[1,5120]{1,0:T(1,128)}, u32[]{:S(2)}) copy-start(s32[1,5120]{1,0:T(1,128)} %param.8) | copy-start | bytes 61444
  0.7 10.7 %copy-start.1 = (s32[1,512]{1,0:T(1,128)S(1)}, s32[1,512]{1,0:T(1,128)}, u32[]{:S(2)}) copy-start(s32[1,512]{1,0:T(1,128)} %param.9) | copy-start | bytes 6148
  3.5 28.4 %collective-permute-start.3 = (f32[3,128]{1,0:T(4,128)S(1)}, f32[3,128]{1,0:T(4,128)S(1)}, u32[]{:S(2)}, u32[]{:S(2)}) collective-permute-start(f32[3,128]{1,0:T(4,128)S(1)} %bitcast.39), channel_id=1, source_target_pairs={{1,0},{0,1},{3,2},{2,3},{5,4},{4,5},{7,6},{6,7},{9,8},{8,9},{11,10... | collective-permute-start | bytes 4616 | tf_op jit(solution)/shard_map/ppermute | solution.py:20
  4.1 27.9 %collective-permute-start.2 = (f32[3,128]{1,0:T(4,128)S(1)}, f32[3,128]{1,0:T(4,128)S(1)}, u32[]{:S(2)}, u32[]{:S(2)}) collective-permute-start(f32[3,128]{1,0:T(4,128)S(1)} %bitcast.40), channel_id=1, source_target_pairs={{1,0},{0,1},{3,2},{2,3},{5,4},{4,5},{7,6},{6,7},{9,8},{8,9},{11,10... | collective-permute-start | bytes 4616 | tf_op jit(solution)/shard_map/ppermute | solution.py:20
  4.2 27.8 %collective-permute-start.1 = (f32[3,128]{1,0:T(4,128)S(1)}, f32[3,128]{1,0:T(4,128)S(1)}, u32[]{:S(2)}, u32[]{:S(2)}) collective-permute-start(f32[3,128]{1,0:T(4,128)S(1)} %bitcast.41), channel_id=1, source_target_pairs={{30,0},{0,2},{2,4},{4,6},{6,8},{8,10},{10,12},{12,14},{14,16},{16,... | collective-permute-start | bytes 4616 | tf_op jit(solution)/shard_map/ppermute | solution.py:20
  7.2 24.8 %collective-permute-start = (f32[3,128]{1,0:T(4,128)S(1)}, f32[3,128]{1,0:T(4,128)S(1)}, u32[]{:S(2)}, u32[]{:S(2)}) collective-permute-start(f32[3,128]{1,0:T(4,128)S(1)} %bitcast.42), channel_id=1, source_target_pairs={{2,0},{4,2},{6,4},{8,6},{10,8},{12,10},{14,12},{16,14},{18,16},{20... | collective-permute-start | bytes 4616 | tf_op jit(solution)/shard_map/ppermute | solution.py:20
  63.6 54.1 %copy-start.3 = (f32[64]{0:T(128)S(1)}, f32[64]{0:T(128)}, u32[]{:S(2)}) copy-start(f32[64]{0:T(128)} %param.11) | copy-start | bytes 772
where the time goes:
time: 135 us
  local copies, waits for them, and re-layouts  56.5 us (42%)
  blocking collectives  38 us (28%)
  other arithmetic  30.7 us (23%)
  starting transfers between devices  7.57 us (6%)
  between operations  1.62 us (1%)
    psum x1, blocking collectives, body(): summed, motion_work = lax.psum((padded, local_energy), ('slab', 'sub'))  38 us
    scatter-add x1, other arithmetic, bin_cells(): return totals.at[:, cells].add(stacked)  27.9 us
    gather x2, local copies, waits for them, and re-layouts, collide(): normal = axes[:, cells]  20.2 us
    gather x2, local copies, waits for them, and re-layouts, body(): relative = speeds - average_value[:, cells]  14.2 us
    gather x2, local copies, waits for them, and re-layouts, collide(): return shifted[:, cells] + speed_multiplier * rotated  14.2 us
    ppermute x4, starting transfers between devices, from_behind(): return lax.ppermute(block, axis, route)  7.57 us
    scatter x2, local copies, waits for them, and re-layouts, body(): speeds = speeds.at[:, slots].set(arriving)  3.44 us
  transfers between devices with their start and end apart: 4, of which 0 were waited for; matrix products, arithmetic and copies ran while one was open for 15% of the time, Pallas kernels for 0%

commit v1 on v0

--- a/solution.py
+++ b/solution.py
@@ -12,6 +12,11 @@
 RESERVOIR_HEAT = 0.9
 FEEDBACK = 1.0
 GOLDEN = 2.399963229728653
+
+
+def axis_by_axis(value, axis_one, axis_two):
+    inner = lax.psum(value, axis_one)
+    return lax.psum(inner, axis_two)
 
 
 def from_behind(block, axis, distance):
@@ -88,7 +93,7 @@
     padded = lax.dynamic_update_slice(
         jnp.zeros((CY * sub_count,), jnp.float32), line_aggregate, (inner_position * CY,)
     )
-    summed, motion_work = lax.psum((padded, local_energy), ("slab", "sub"))
+    summed, motion_work = axis_by_axis((padded, local_energy), "sub", "slab")
     column_sum = lax.dynamic_slice(summed, (inner_position * CY,), (CY,))
     speed_multiplier = lax.rsqrt(motion_work / (3.0 * whole_swarm * RESERVOIR_HEAT) + 1e-06)
     adjustment_factor = FEEDBACK * (shear_target - column_sum / width_x)

time: 135 us -> 139 us (1.030)
  blocking collectives: 38 us -> 42.3 us
    psum x1 -> x2, blocking collectives: 38 us -> 42.3 us  [the longest x1 39.2 us: axis_by_axis(): return lax.psum(inner, axis_two)]
where the time goes in v1:
time: 139 us
  local copies, waits for them, and re-layouts  56.5 us (41%)
  blocking collectives  42.3 us (30%)
  other arithmetic  30.7 us (22%)
  starting transfers between devices  7.57 us (5%)
  between operations  1.62 us (1%)
    psum x1, blocking collectives, axis_by_axis(): return lax.psum(inner, axis_two)  39.2 us
    scatter-add x1, other arithmetic, bin_cells(): return totals.at[:, cells].add(stacked)  27.9 us
    gather x2, local copies, waits for them, and re-layouts, collide(): normal = axes[:, cells]  20.2 us
    gather x2, local copies, waits for them, and re-layouts, body(): relative = speeds - average_value[:, cells]  14.2 us
    gather x2, local copies, waits for them, and re-layouts, collide(): return shifted[:, cells] + speed_multiplier * rotated  14.2 us
    ppermute x4, starting transfers between devices, from_behind(): return lax.ppermute(block, axis, route)  7.57 us
    scatter x2, local copies, waits for them, and re-layouts, body(): speeds = speeds.at[:, slots].set(arriving)  3.44 us
    psum x1, blocking collectives, axis_by_axis(): inner = lax.psum(value, axis_one)  3.08 us
  transfers between devices with their start and end apart: 4, of which 0 were waited for; matrix products, arithmetic and copies ran while one was open for 15% of the time, Pallas kernels for 0%

profile of v1, /device:TPU:0, one launch (start us, length us, event | category | flops | bytes accessed | tf_op | source)
XLA Modules:
  0.0 139.0 jit_solution(18188697162355460351)
XLA Ops:
  0.7 1.7 %copy.103 = f32[3,5120]{0,1:T(8,128)S(1)} copy(f32[3,5120]{1,0:T(4,128)} %param.7) | data formatting | bytes 122880 | tf_op args[0]
  2.4 1.0 gather_fusion
  3.5 0.5 collective-permute-start.3
  4.2 3.0 %collective-permute-start.1 = (f32[3,128]{1,0:T(4,128)S(1)}, f32[3,128]{1,0:T(4,128)S(1)}, u32[]{:S(2)}, u32[]{:S(2)}) collective-permute-start(f32[3,128]{1,0:T(4,128)S(1)} %bitcast.41), channel_id=1, source_target_pairs={{30,0},{0,2},{2,4},{4,6},{6,8},{8,10},{10,12},{12,14},{14,16},{16,... | collective-permute-start | bytes 4616 | tf_op jit(solution)/shard_map/ppermute | solution.py:25
  7.2 4.0 %collective-permute-start = (f32[3,128]{1,0:T(4,128)S(1)}, f32[3,128]{1,0:T(4,128)S(1)}, u32[]{:S(2)}, u32[]{:S(2)}) collective-permute-start(f32[3,128]{1,0:T(4,128)S(1)} %bitcast.42), channel_id=1, source_target_pairs={{2,0},{4,2},{6,4},{8,6},{10,8},{12,10},{14,12},{16,14},{18,16},{20... | collective-permute-start | bytes 4616 | tf_op jit(solution)/shard_map/ppermute | solution.py:25
  11.4 0.4 fusion.5
  11.8 17.7 %gather_fusion.3 = f32[5120,3]{1,0:T(8,128)} fusion(f32[3,512]{0,1:T(8,128)S(1)} %fusion.5, s32[5120]{0:T(1024)S(1)} %broadcast_clamp_fusion), kind=kCustom, calls=%fused_computation.3 | custom fusion | bytes 143360 | tf_op jit(solution)/shard_map/gather | solution.py:53
  29.4 2.5 %copy.111 = f32[5120,3]{0,1:T(4,128)S(1)} copy(f32[5120,3]{1,0:T(8,128)} %gather_fusion.3) | data formatting | bytes 122880 | tf_op jit(solution)/shard_map/gather | solution.py:53
  32.0 0.1 copy.113
  32.2 2.7 %scatter_fusion = f32[3,5120]{0,1:T(8,128)S(1)} fusion(f32[3,5120]{0,1:T(8,128)S(1)} %copy.103, s32[512]{0:T(512)S(1)} %bitcast.37, f32[512,3]{1,0:T(8,128)S(1)} %bitcast.33), kind=kCustom, calls=%fused_computation.4 | custom fusion | bytes 20480 | tf_op jit(solution)/shard_map/scatter | solution.py:87
  34.9 0.8 copy.109
  35.6 27.9 %scatter_custom_fusion.1 = f32[4,512]{0,1:T(8,128)S(1)} fusion(s32[5120]{0:T(1024)S(1)} %bitcast.35, f32[3,5120]{0,1:T(8,128)S(1)} %scatter_fusion, f32[]{:T(128)} %constant.59.clone.1, f32[]{:T(128)} %constant.55.clone.1), kind=kCustom, calls=%fused_computation.6 | custom fusion | flops 20480 | bytes 2629640 | tf_op jit(solution)/shard_map/scatter-add | solution.py:39
  63.6 0.2 fusion.3
  63.8 0.1 bitcast_reduce_fusion
  63.9 0.1 slice_divide_fusion
  64.0 13.4 %gather_fusion.2 = f32[5120,3]{1,0:T(8,128)S(1)} fusion(f32[3,512]{0,1:T(8,128)S(1)} %slice_divide_fusion, s32[5120]{0:T(1024)S(1)} %broadcast_clamp_fusion), kind=kCustom, calls=%fused_computation.2 | custom fusion | bytes 143360 | tf_op jit(solution)/shard_map/gather | solution.py:90
  77.5 0.8 copy.108
  78.3 0.1 fusion.18
  78.3 0.1 copy.118
  78.4 0.1 copy.119
  78.5 0.7 multiply_reduce_fusion.1
  79.2 0.5 bitcast_dynamic-update-slice_fusion
  79.7 3.1 %all-reduce.2 = (f32[128]{0:T(128)S(1)}, f32[]{:T(128)}) all-reduce(f32[128]{0:T(128)S(1)} %get-tuple-element.31, f32[]{:T(128)} %get-tuple-element.24), channel_id=1, replica_groups=mesh['slab'=16,'sub'=2] {'sub'}, use_global_device_ids=true, to_apply=%region_3.0 | all-reduce | flops 129 | bytes 1032 | tf_op jit(solution)/shard_map/psum | solution.py:18
  82.8 39.2 %all-reduce.1 = (f32[128]{0:T(128)S(1)}, f32[]{:T(128)}) all-reduce(f32[128]{0:T(128)S(1)} %get-tuple-element.28, f32[]{:T(128)} %get-tuple-element.29), channel_id=1, replica_groups=mesh['slab'=16,'sub'=2] {'slab'}, use_global_device_ids=true, to_apply=%region_4.0 | all-reduce | flops 129 | bytes 1032 | tf_op jit(solution)/shard_map/psum | solution.py:19
  122.0 0.1 multiply_subtract_fusion.4
  122.1 0.1 broadcast_in_dim.10
  122.1 0.1 broadcast_in_dim.12
  122.3 0.9 scatter-add.13
  123.2 13.4 %gather_fusion.1 = f32[5120,3]{1,0:T(8,128)S(1)} fusion(f32[3,512]{0,1:T(8,128)S(1)} %scatter-add.13, s32[5120]{0:T(1024)S(1)} %broadcast_clamp_fusion), kind=kCustom, calls=%fused_computation.1 | custom fusion | bytes 143360 | tf_op jit(solution)/shard_map/gather | solution.py:64
  136.7 0.8 copy.107
  138.1 0.1 multiply_subtract_fusion.2
  138.2 0.7 fusion.9
  (32 shorter events, 0.5 us)
Async XLA Ops:
  0.6 1.7 %copy-start.2 = (s32[1,4,128]{2,1,0:T(4,128)S(1)}, s32[1,4,128]{2,1,0:T(4,128)}, u32[]{:S(2)}) copy-start(s32[1,4,128]{2,1,0:T(4,128)} %param.10) | copy-start | bytes 6148
  0.6 10.7 %copy-start = (s32[1,5120]{1,0:T(1,128)S(1)}, s32[1,5120]{1,0:T(1,128)}, u32[]{:S(2)}) copy-start(s32[1,5120]{1,0:T(1,128)} %param.8) | copy-start | bytes 61444
  0.7 10.7 %copy-start.1 = (s32[1,512]{1,0:T(1,128)S(1)}, s32[1,512]{1,0:T(1,128)}, u32[]{:S(2)}) copy-start(s32[1,512]{1,0:T(1,128)} %param.9) | copy-start | bytes 6148
  3.5 28.4 %collective-permute-start.3 = (f32[3,128]{1,0:T(4,128)S(1)}, f32[3,128]{1,0:T(4,128)S(1)}, u32[]{:S(2)}, u32[]{:S(2)}) collective-permute-start(f32[3,128]{1,0:T(4,128)S(1)} %bitcast.39), channel_id=1, source_target_pairs={{1,0},{0,1},{3,2},{2,3},{5,4},{4,5},{7,6},{6,7},{9,8},{8,9},{11,10... | collective-permute-start | bytes 4616 | tf_op jit(solution)/shard_map/ppermute | solution.py:25
  4.1 27.9 %collective-permute-start.2 = (f32[3,128]{1,0:T(4,128)S(1)}, f32[3,128]{1,0:T(4,128)S(1)}, u32[]{:S(2)}, u32[]{:S(2)}) collective-permute-start(f32[3,128]{1,0:T(4,128)S(1)} %bitcast.40), channel_id=1, source_target_pairs={{1,0},{0,1},{3,2},{2,3},{5,4},{4,5},{7,6},{6,7},{9,8},{8,9},{11,10... | collective-permute-start | bytes 4616 | tf_op jit(solution)/shard_map/ppermute | solution.py:25
  4.2 27.8 %collective-permute-start.1 = (f32[3,128]{1,0:T(4,128)S(1)}, f32[3,128]{1,0:T(4,128)S(1)}, u32[]{:S(2)}, u32[]{:S(2)}) collective-permute-start(f32[3,128]{1,0:T(4,128)S(1)} %bitcast.41), channel_id=1, source_target_pairs={{30,0},{0,2},{2,4},{4,6},{6,8},{8,10},{10,12},{12,14},{14,16},{16,... | collective-permute-start | bytes 4616 | tf_op jit(solution)/shard_map/ppermute | solution.py:25
  7.2 24.8 %collective-permute-start = (f32[3,128]{1,0:T(4,128)S(1)}, f32[3,128]{1,0:T(4,128)S(1)}, u32[]{:S(2)}, u32[]{:S(2)}) collective-permute-start(f32[3,128]{1,0:T(4,128)S(1)} %bitcast.42), channel_id=1, source_target_pairs={{2,0},{4,2},{6,4},{8,6},{10,8},{12,10},{14,12},{16,14},{18,16},{20... | collective-permute-start | bytes 4616 | tf_op jit(solution)/shard_map/ppermute | solution.py:25
  63.6 58.4 %copy-start.3 = (f32[64]{0:T(128)S(1)}, f32[64]{0:T(128)}, u32[]{:S(2)}) copy-start(f32[64]{0:T(128)} %param.11) | copy-start | bytes 772
